TPU v7x, 32 devices: a whole 2x2x4 slice. The times are simulated.
32 devices in a mesh: dp: 4 (over z), mp: 8 (over y, x, core).
Axes of the slice: x: 2, y: 2, z: 4, core: 2. Of those that a mesh axis runs over, the one named last changes fastest.
Arguments:
- behaviors: bfloat16 [32, 2048, 1024], P('dp', 'mp'), may hold values from -8 to 8
- candidates: bfloat16 [32, 2048, 128], P('dp', 'mp'), may hold values from -12 to 12
- lengths: int32 [32], P('dp'), may hold values from 128 to 1024
- bilinear: bfloat16 [2048, 2048], P('mp'), may hold values from -1 to 2
- norm_gain: float32 [2048], replicated, may hold values from 0.1 to 1.9
- w_gate: bfloat16 [2048, 8192], P('dp', 'mp'), may hold values from -0.125 to 0.125
- w_up: bfloat16 [2048, 8192], P('dp', 'mp'), may hold values from -0.125 to 0.125
- w_down: bfloat16 [8192, 2048], P('mp', 'dp'), may hold values from -0.0625 to 0.0625
Outputs:
- interest: bfloat16 [32, 2048, 128], P('dp', 'mp')
All inputs are finite; a program needn't handle non-finite values.
Results may differ from a plain program's by a relative error of at most 0.015.
Values may be sent and summed in bfloat16 or wider, within the bound.
No kernel may reach another device: no remote copies, remote signals or barrier semaphores. Data moves between devices by JAX's collectives and lax.ppermute only.
A program may use at most 64 MiB of HBM per device.

v0:
```python
import math
import jax
import jax.numpy as jnp
from jax import lax
from jax.sharding import PartitionSpec as P


def attention_weights(scores, live):
    masked = jnp.where(live, scores, -1e30)
    highest = jnp.max(masked, axis=-1, keepdims=True)
    expons = jnp.where(live, jnp.exp(masked - highest), 0.0)
    return (expons / jnp.sum(expons, axis=-1, keepdims=True)).astype(jnp.bfloat16)


def shards(behaviors, candidates, lengths, bilinear, norm_gain, w_gate, w_up, w_down):
    user_count, width_part, cand_count = candidates.shape
    feature_width = bilinear.shape[1]
    behavior_count = behaviors.shape[2]
    query_part = jnp.einsum(
        "ek,ukc->uec",
        bilinear,
        lax.all_gather(candidates, "mp", axis=1, tiled=True),
        preferred_element_type=jnp.float32,
    )
    query = query_part.astype(jnp.bfloat16)
    partial_value = jnp.einsum("ukc,ukl->ucl", query, behaviors, preferred_element_type=jnp.float32)
    scale = 1.0 / math.sqrt(feature_width)
    live = (
        lax.broadcasted_iota(jnp.int32, (user_count, 1, behavior_count), 2) < lengths[:, None, None]
    )
    share = lax.psum_scatter(partial_value, "mp", scatter_dimension=1, tiled=True)
    probs_share = attention_weights(share * scale, live)
    probs = lax.all_gather(probs_share, "mp", axis=1, tiled=True)
    pooled = jnp.einsum(
        "ucl,ukl->ukc", probs, behaviors, preferred_element_type=jnp.float32
    ).astype(jnp.bfloat16)
    whole = lax.all_gather(pooled, "mp", axis=1, tiled=True)
    values = whole.astype(jnp.float32)
    square_mean = jnp.mean(values * values, axis=1, keepdims=True)
    normed = (values * lax.rsqrt(square_mean + 1e-06) * norm_gain[None, :, None]).astype(
        jnp.bfloat16
    )
    gate = jnp.einsum(
        "ukc,kf->ucf",
        normed,
        lax.all_gather(w_gate, "dp", axis=0, tiled=True),
        preferred_element_type=jnp.float32,
    )
    upward = jnp.einsum(
        "ukc,kf->ucf",
        normed,
        lax.all_gather(w_up, "dp", axis=0, tiled=True),
        preferred_element_type=jnp.float32,
    )
    hidden = (jax.nn.silu(gate) * upward).astype(jnp.bfloat16)
    down_full = lax.all_gather(w_down, "dp", axis=1, tiled=True)
    result = lax.psum_scatter(
        jnp.einsum("ucf,fk->kuc", hidden, down_full, preferred_element_type=jnp.float32).astype(
            jnp.bfloat16
        ),
        "mp",
        scatter_dimension=0,
        tiled=True,
    ).astype(jnp.float32)
    return jnp.transpose(result, (1, 0, 2)).astype(jnp.bfloat16)


def solution(mesh):
    return jax.shard_map(
        shards,
        mesh=mesh,
        in_specs=(
            P("dp", "mp", None),
            P("dp", "mp", None),
            P("dp"),
            P("mp", None),
            P(),
            P("dp", "mp"),
            P("dp", "mp"),
            P("mp", "dp"),
        ),
        out_specs=P("dp", "mp", None),
        check_vma=False,
    )
```

profile of v0, /device:TPU:0, one launch (start us, length us, event | category | flops | bytes accessed | tf_op | source)
XLA Modules:
  0.0 498.7 jit_solution(1023455317639719504)
XLA Ops:
  6.5 0.7 all-gather.7.cloned.1.call-update
  7.3 41.3 %all-gather.7.cloned.1.call-done = bf16[8,2048,128]{2,1,0:T(8,128)(2,1)} async-done(((bf16[8,256,128]{2,1,0:T(8,128)(2,1)}), bf16[8,2048,128]{2,1,0:T(8,128)(2,1)}) %all-gather.7.cloned.1.call-update) | async-done | bytes 4194320 | tf_op jit(solution)/shard_map/all_gather | solution.py:22
  48.6 8.2 %fusion.24 = f32[8,128,1024]{2,1,0:T(8,128)} fusion(bf16[8,256,1024]{2,1,0:T(8,128)(2,1)} %param.8, bf16[8,2048,128]{2,1,0:T(8,128)(2,1)} %all-gather.7.cloned.1.call-done, bf16[256,2048]{1,0:T(8,128)(2,1)S(1)} %copy-done), kind=kOutput, calls=%fused_computation.18 | convolution fusion | flops 1610874880 | bytes 13631488 | tf_op jit(solution)/shard_map/ukc,ukl->ucl/dot_general | solution.py:26
  56.8 0.0 all-gather.9.cloned.1.call-start
  56.8 0.6 copy-done.1
  57.4 0.1 iota_compare_fusion
  57.5 50.5 %reduce-scatter.3.cloned.1.call-done = f32[8,16,1024]{2,1,0:T(8,128)} async-done(((f32[8,128,1024]{2,1,0:T(8,128)}), f32[8,16,1024]{2,1,0:T(8,128)}) %reduce-scatter.3.cloned.1.call-update) | async-done | bytes 524304 | tf_op jit(solution)/shard_map/reduce_scatter | solution.py:31
  108.0 1.7 fusion.37
  109.7 0.8 divide_convert_fusion
  110.6 27.9 %all-gather.9.cloned.1.call-done = bf16[8,128,1024]{2,1,0:T(8,128)(2,1)} async-done(((bf16[8,16,1024]{2,1,0:T(8,128)(2,1)}), bf16[8,128,1024]{2,1,0:T(8,128)(2,1)}) %all-gather.9.cloned.1.call-update) | async-done | bytes 2097168 | tf_op jit(solution)/shard_map/all_gather | solution.py:33
  138.5 5.2 %fusion.27 = bf16[8,256,128]{1,2,0:T(8,128)(2,1)} fusion(bf16[8,128,1024]{2,1,0:T(8,128)(2,1)} %all-gather.9.cloned.1.call-done, bf16[8,256,1024]{2,1,0:T(8,128)(2,1)} %param.8), kind=kOutput, calls=%fused_computation.21 | convolution fusion | flops 537133056 | bytes 6815744 | tf_op jit(solution)/shard_map/ucl,ukl->ukc/dot_general | solution.py:34
  143.7 0.5 all-gather.13.cloned.1.call-update
  144.3 0.5 all-gather.15.cloned.1.call-update
  144.9 0.7 all-gather.17.cloned.1.call-update
  145.6 0.2 reduce-scatter.5.cloned.1.call-start
  145.8 35.4 %all-gather.11.cloned.1.call-done = bf16[8,2048,128]{1,2,0:T(8,128)(2,1)} async-done(((bf16[8,256,128]{1,2,0:T(8,128)(2,1)}), bf16[8,2048,128]{1,2,0:T(8,128)(2,1)}) %all-gather.11.cloned.1.call-update) | async-done | bytes 4194320 | tf_op jit(solution)/shard_map/all_gather | solution.py:37
  181.2 3.1 fusion.1
  184.3 79.1 %all-gather.13.cloned.1.call-done = bf16[2048,1024]{1,0:T(8,128)(2,1)} async-done(((bf16[512,1024]{1,0:T(8,128)(2,1)}), bf16[2048,1024]{1,0:T(8,128)(2,1)}) %all-gather.13.cloned.1.call-update) | async-done | bytes 4194320 | tf_op jit(solution)/shard_map/all_gather | solution.py:46
  263.4 9.9 %fusion.8 = f32[8,128,1024]{2,1,0:T(8,128)} fusion(bf16[2048,1024]{1,0:T(8,128)(2,1)} %all-gather.13.cloned.1.call-done, bf16[8,2048,128]{1,2,0:T(8,128)(2,1)} %all-gather.11.cloned.1.call-done, f32[2048]{0:T(1024)S(1)} %copy-done.2, f32[8,128]{1,0:T(8,128)S(1)} %add_rsqrt_fusion), kind=kOutput, calls=%fused_computation.10 | convolution fusion | flops 4303355904 | bytes 12595200 | tf_op jit(solution)/shard_map/ukc,kf->ucf/dot_general | solution.py:43
  273.3 70.7 %all-gather.15.cloned.1.call-done = bf16[2048,1024]{1,0:T(8,128)(2,1)} async-done(((bf16[512,1024]{1,0:T(8,128)(2,1)}), bf16[2048,1024]{1,0:T(8,128)(2,1)}) %all-gather.15.cloned.1.call-update) | async-done | bytes 4194320 | tf_op jit(solution)/shard_map/all_gather | solution.py:52
  344.0 80.8 %all-gather.17.cloned.1.call-done = bf16[1024,2048]{1,0:T(8,128)(2,1)} async-done(((bf16[1024,512]{1,0:T(8,128)(2,1)}), bf16[1024,2048]{1,0:T(8,128)(2,1)}) %all-gather.17.cloned.1.call-update) | async-done | bytes 4194320 | tf_op jit(solution)/shard_map/all_gather | solution.py:56
  424.9 15.2 %convert_bitcast_fusion = bf16[2048,8,128]{0,2,1:T(8,128)(2,1)} fusion(bf16[1024,2048]{1,0:T(8,128)(2,1)} %all-gather.17.cloned.1.call-done, f32[8,128,1024]{2,1,0:T(8,128)} %fusion.8, bf16[2048,1024]{1,0:T(8,128)(2,1)} %all-gather.15.cloned.1.call-done, bf16[8,2048,128]{1,2,0:T(8,128)(2,1)} %all-gather.11.cloned.1.call-done, f32[2048]{0:T(1024)S(1)} %copy-done.2, ...), kind=kOutput, calls=%fused_computation.12 | convolution fusion | flops 8606711808 | bytes 20983808 | tf_op jit(solution)/shard_map/ucf,fk->kuc/dot_general | solution.py:58
  440.1 49.7 %reduce-scatter.5.cloned.1.call-done = bf16[256,8,128]{0,2,1:T(8,128)(2,1)} async-done(((bf16[2048,8,128]{0,2,1:T(8,128)(2,1)}), bf16[256,8,128]{0,2,1:T(8,128)(2,1)}) %reduce-scatter.5.cloned.1.call-update) | async-done | bytes 524304 | tf_op jit(solution)/shard_map/reduce_scatter | solution.py:57
  489.8 2.0 copy.9
  (16 shorter events, 0.3 us)
Async XLA Ops:
  6.5 42.0 %copy-start = (bf16[256,2048]{1,0:T(8,128)(2,1)S(1)}, bf16[256,2048]{1,0:T(8,128)(2,1)}, u32[]{:S(2)}) copy-start(bf16[256,2048]{1,0:T(8,128)(2,1)} %param.11) | copy-start | bytes 3145732
  6.5 42.0 %all-gather.7.cloned.1.call-start = ((), (), s32[]{:S(2)}) async-start(), calls=%async_computation.2 | async-start | bytes 4718592 | tf_op jit(solution)/shard_map/all_gather | solution.py:22
  7.3 100.8 %reduce-scatter.3.cloned.1.call-start = ((), (), s32[]{:S(2)}) async-start(), calls=%async_computation.3 | async-start | bytes 4718592 | tf_op jit(solution)/shard_map/reduce_scatter | solution.py:31
  56.7 0.7 copy-start.1
  56.8 81.7 %all-gather.9.cloned.1.call-start = ((), (), s32[]{:S(2)}) async-start(), calls=%async_computation.4 | async-start | bytes 2359296 | tf_op jit(solution)/shard_map/all_gather | solution.py:33
  110.6 70.6 %all-gather.11.cloned.1.call-start = ((), (), s32[]{:S(2)}) async-start(), calls=%async_computation.5 | async-start | bytes 4718592 | tf_op jit(solution)/shard_map/all_gather | solution.py:37
  143.7 119.7 %copy-start.2 = (f32[2048]{0:T(1024)S(1)}, f32[2048]{0:T(1024)}, u32[]{:S(2)}) copy-start(f32[2048]{0:T(1024)} %param.12) | copy-start | bytes 24580
  143.7 119.7 %all-gather.13.cloned.1.call-start = ((), (), s32[]{:S(2)}) async-start(), calls=%async_computation.6 | async-start | bytes 5242880 | tf_op jit(solution)/shard_map/all_gather | solution.py:46
  144.3 199.8 %all-gather.15.cloned.1.call-start = ((), (), s32[]{:S(2)}) async-start(), calls=%async_computation.7 | async-start | bytes 5242880 | tf_op jit(solution)/shard_map/all_gather | solution.py:52
  144.8 280.0 %all-gather.17.cloned.1.call-start = ((), (), s32[]{:S(2)}) async-start(), calls=%async_computation.8 | async-start | bytes 5242880 | tf_op jit(solution)/shard_map/all_gather | solution.py:56
  145.6 344.2 %reduce-scatter.5.cloned.1.call-start = ((), (), s32[]{:S(2)}) async-start(), calls=%async_computation.9 | async-start | bytes 4718592 | tf_op jit(solution)/shard_map/reduce_scatter | solution.py:57
Sparse Core Ops, SparseCore 0:
  9.2 39.2 all-gather.6
  56.9 51.0 reduce-scatter.2
  110.7 27.7 all-gather.8
  143.8 37.3 all-gather.10
  182.6 80.7 all-gather.12
  264.8 79.2 all-gather.14
  345.6 79.2 all-gather.16
  440.2 49.5 reduce-scatter.4
where the time goes:
time: 499 us
  waiting for transfers between devices  438 us (88%)
  matrix products  38.4 us (8%)
  between operations  13.5 us (3%)
  other arithmetic  5.68 us (1%)
    all_gather x1, waiting for transfers between devices, shards(): down_full = lax.all_gather(w_down, 'dp', axis=1, tiled=True)  80.8 us
    all_gather x1, waiting for transfers between devices, shards(): lax.all_gather(w_gate, 'dp', axis=0, tiled=True)  79.1 us
    all_gather x1, waiting for transfers between devices, shards(): lax.all_gather(w_up, 'dp', axis=0, tiled=True)  70.7 us
    reduce_scatter x1, waiting for transfers between devices, shards(): lax.psum_scatter(partial_value, 'mp', scatter_dimension=1, tiled=True)  50.5 us
    reduce_scatter x1, waiting for transfers between devices, shards(): lax.psum_scatter(jnp.einsum('ucf,fk->kuc', hidden, down_full, preferred_e...  49.7 us
    all_gather x1, waiting for transfers between devices, shards(): lax.all_gather(candidates, 'mp', axis=1, tiled=True)  41.3 us
    all_gather x1, waiting for transfers between devices, shards(): whole = lax.all_gather(pooled, 'mp', axis=1, tiled=True)  35.4 us
    all_gather x1, waiting for transfers between devices, shards(): probs = lax.all_gather(probs_share, 'mp', axis=1, tiled=True)  27.9 us
  transfers between devices with their start and end apart: 8, of which 8 were waited for; matrix products, arithmetic and copies ran while one was open for 3% of the time, Pallas kernels for 0%

commit v1 on v0

--- a/solution.py
+++ b/solution.py
@@ -16,12 +16,27 @@
     user_count, width_part, cand_count = candidates.shape
     feature_width = bilinear.shape[1]
     behavior_count = behaviors.shape[2]
-    query_part = jnp.einsum(
+    size, index = (lax.axis_size("mp"), lax.axis_index("mp"))
+    backward = [(i, (i - 1) % size) for i in range(size)]
+    rows = candidates.shape[1]
+    carried = candidates
+    total = jnp.einsum(
         "ek,ukc->uec",
-        bilinear,
-        lax.all_gather(candidates, "mp", axis=1, tiled=True),
+        lax.dynamic_slice_in_dim(bilinear, index * rows, carried.shape[1], axis=1),
+        carried,
         preferred_element_type=jnp.float32,
     )
+    for step in range(1, size):
+        carried = lax.ppermute(carried, "mp", backward)
+        total = total + jnp.einsum(
+            "ek,ukc->uec",
+            lax.dynamic_slice_in_dim(
+                bilinear, (index + step) % size * rows, carried.shape[1], axis=1
+            ),
+            carried,
+            preferred_element_type=jnp.float32,
+        )
+    query_part = total
     query = query_part.astype(jnp.bfloat16)
     partial_value = jnp.einsum("ukc,ukl->ucl", query, behaviors, preferred_element_type=jnp.float32)
     scale = 1.0 / math.sqrt(feature_width)

time: 499 us -> 523 us (1.048)
  starting transfers between devices: 0.46 us -> 20.5 us
    ppermute x0 -> x7, waiting for transfers between devices: none -> 43.7 us  [shards(): carried = lax.ppermute(carried, 'mp', backward)]
    all_gather x1 -> x0, waiting for transfers between devices: 41.3 us -> none  [shards(): lax.all_gather(candidates, 'mp', axis=1, tiled=True)]
    ppermute x0 -> x7, starting transfers between devices: none -> 20.1 us  [shards(): carried = lax.ppermute(carried, 'mp', backward)]
  transfers between devices with their start and end apart: 8 -> 14, of which waited for: 8 -> 14; matrix products, arithmetic and copies ran while one was open for 3% -> 3% of each run, Pallas kernels for 0% -> 0%
where the time goes in v1:
time: 523 us; the launch traced here: 522 us
  waiting for transfers between devices  441 us (84%)
  matrix products  39 us (7%)
  starting transfers between devices  20.5 us (4%)
  between operations  13.6 us (3%)
  other arithmetic  5.65 us (1%)
    all_gather x1, waiting for transfers between devices, shards(): down_full = lax.all_gather(w_down, 'dp', axis=1, tiled=True)  80.7 us
    all_gather x1, waiting for transfers between devices, shards(): lax.all_gather(w_gate, 'dp', axis=0, tiled=True)  79.1 us
    all_gather x1, waiting for transfers between devices, shards(): lax.all_gather(w_up, 'dp', axis=0, tiled=True)  70.7 us
    reduce_scatter x1, waiting for transfers between devices, shards(): lax.psum_scatter(partial_value, 'mp', scatter_dimension=1, tiled=True)  52.2 us
    reduce_scatter x1, waiting for transfers between devices, shards(): lax.psum_scatter(jnp.einsum('ucf,fk->kuc', hidden, down_full, preferred_e...  49.7 us
    ppermute x7, waiting for transfers between devices, shards(): carried = lax.ppermute(carried, 'mp', backward)  43.7 us
    all_gather x1, waiting for transfers between devices, shards(): whole = lax.all_gather(pooled, 'mp', axis=1, tiled=True)  35.5 us
    all_gather x1, waiting for transfers between devices, shards(): probs = lax.all_gather(probs_share, 'mp', axis=1, tiled=True)  27.9 us
  transfers between devices with their start and end apart: 14, of which 14 were waited for; matrix products, arithmetic and copies ran while one was open for 3% of the time, Pallas kernels for 0%

profile of v1, /device:TPU:0, one launch (start us, length us, event | category | flops | bytes accessed | tf_op | source)
XLA Modules:
  0.0 522.4 jit_solution(1747723572038536245)
XLA Ops:
  6.5 3.4 collective-permute-start
  9.9 7.0 %collective-permute-done = bf16[8,256,128]{2,1,0:T(8,128)(2,1)S(1)} collective-permute-done((bf16[8,256,128]{2,1,0:T(8,128)(2,1)}, bf16[8,256,128]{2,1,0:T(8,128)(2,1)S(1)}, u32[]{:S(2)}, u32[]{:S(2)}) %collective-permute-start) | collective-permute-done | bytes 524320 | tf_op jit(solution)/shard_map/ppermute | solution.py:30
  19.6 6.7 %collective-permute-done.1 = bf16[8,256,128]{2,1,0:T(8,128)(2,1)S(1)} collective-permute-done((bf16[8,256,128]{2,1,0:T(8,128)(2,1)S(1)}, bf16[8,256,128]{2,1,0:T(8,128)(2,1)S(1)}, u32[]{:S(2)}, u32[]{:S(2)}) %collective-permute-start.1) | collective-permute-done | bytes 524320 | tf_op jit(solution)/shard_map/ppermute | solution.py:30
  26.3 2.8 collective-permute-start.2
  29.1 6.7 %collective-permute-done.2 = bf16[8,256,128]{2,1,0:T(8,128)(2,1)S(1)} collective-permute-done((bf16[8,256,128]{2,1,0:T(8,128)(2,1)S(1)}, bf16[8,256,128]{2,1,0:T(8,128)(2,1)S(1)}, u32[]{:S(2)}, u32[]{:S(2)}) %collective-permute-start.2) | collective-permute-done | bytes 524320 | tf_op jit(solution)/shard_map/ppermute | solution.py:30
  35.8 2.8 collective-permute-start.3
  40.0 5.3 %collective-permute-done.3 = bf16[8,256,128]{2,1,0:T(8,128)(2,1)S(1)} collective-permute-done((bf16[8,256,128]{2,1,0:T(8,128)(2,1)S(1)}, bf16[8,256,128]{2,1,0:T(8,128)(2,1)S(1)}, u32[]{:S(2)}, u32[]{:S(2)}) %collective-permute-start.3) | collective-permute-done | bytes 524320 | tf_op jit(solution)/shard_map/ppermute | solution.py:30
  45.3 2.8 collective-permute-start.4
  48.9 6.0 %collective-permute-done.4 = bf16[8,256,128]{2,1,0:T(8,128)(2,1)S(1)} collective-permute-done((bf16[8,256,128]{2,1,0:T(8,128)(2,1)S(1)}, bf16[8,256,128]{2,1,0:T(8,128)(2,1)S(1)}, u32[]{:S(2)}, u32[]{:S(2)}) %collective-permute-start.4) | collective-permute-done | bytes 524320 | tf_op jit(solution)/shard_map/ppermute | solution.py:30
  54.8 2.8 collective-permute-start.5
  58.4 6.0 %collective-permute-done.5 = bf16[8,256,128]{2,1,0:T(8,128)(2,1)S(1)} collective-permute-done((bf16[8,256,128]{2,1,0:T(8,128)(2,1)S(1)}, bf16[8,256,128]{2,1,0:T(8,128)(2,1)S(1)}, u32[]{:S(2)}, u32[]{:S(2)}) %collective-permute-start.5) | collective-permute-done | bytes 524320 | tf_op jit(solution)/shard_map/ppermute | solution.py:30
  67.9 6.0 %collective-permute-done.6 = bf16[8,256,128]{2,1,0:T(8,128)(2,1)S(1)} collective-permute-done((bf16[8,256,128]{2,1,0:T(8,128)(2,1)S(1)}, bf16[8,256,128]{2,1,0:T(8,128)(2,1)S(1)}, u32[]{:S(2)}, u32[]{:S(2)}) %collective-permute-start.6) | collective-permute-done | bytes 524320 | tf_op jit(solution)/shard_map/ppermute | solution.py:30
  73.8 5.2 fusion.28
  79.8 52.2 %reduce-scatter.3.cloned.1.call-done = f32[8,16,1024]{2,1,0:T(8,128)} async-done(((f32[8,128,1024]{2,1,0:T(8,128)}), f32[8,16,1024]{2,1,0:T(8,128)}) %reduce-scatter.3.cloned.1.call-update) | async-done | bytes 524304 | tf_op jit(solution)/shard_map/reduce_scatter | solution.py:46
  134.5 27.9 %all-gather.6.cloned.1.call-done = bf16[8,128,1024]{2,1,0:T(8,128)(2,1)} async-done(((bf16[8,16,1024]{2,1,0:T(8,128)(2,1)}), bf16[8,128,1024]{2,1,0:T(8,128)(2,1)}) %all-gather.6.cloned.1.call-update) | async-done | bytes 2097168 | tf_op jit(solution)/shard_map/all_gather | solution.py:48
  162.4 5.1 fusion.29
  169.6 35.5 %all-gather.8.cloned.1.call-done = bf16[8,2048,128]{1,2,0:T(8,128)(2,1)} async-done(((bf16[8,256,128]{1,2,0:T(8,128)(2,1)}), bf16[8,2048,128]{1,2,0:T(8,128)(2,1)}) %all-gather.8.cloned.1.call-update) | async-done | bytes 4194320 | tf_op jit(solution)/shard_map/all_gather | solution.py:52
  205.1 3.1 fusion.1
  208.2 79.1 %all-gather.10.cloned.1.call-done = bf16[2048,1024]{1,0:T(8,128)(2,1)} async-done(((bf16[512,1024]{1,0:T(8,128)(2,1)}), bf16[2048,1024]{1,0:T(8,128)(2,1)}) %all-gather.10.cloned.1.call-update) | async-done | bytes 4194320 | tf_op jit(solution)/shard_map/all_gather | solution.py:61
  287.3 9.9 %fusion.8 = f32[8,128,1024]{2,1,0:T(8,128)} fusion(bf16[2048,1024]{1,0:T(8,128)(2,1)} %all-gather.10.cloned.1.call-done, bf16[8,2048,128]{1,2,0:T(8,128)(2,1)} %all-gather.8.cloned.1.call-done, f32[2048]{0:T(1024)S(1)} %copy-done.2, f32[8,128]{1,0:T(8,128)S(1)} %add_rsqrt_fusion), kind=kOutput, calls=%fused_computation.10 | convolution fusion | flops 4303355904 | bytes 12595200 | tf_op jit(solution)/shard_map/ukc,kf->ucf/dot_general | solution.py:58
  297.2 70.7 %all-gather.12.cloned.1.call-done = bf16[2048,1024]{1,0:T(8,128)(2,1)} async-done(((bf16[512,1024]{1,0:T(8,128)(2,1)}), bf16[2048,1024]{1,0:T(8,128)(2,1)}) %all-gather.12.cloned.1.call-update) | async-done | bytes 4194320 | tf_op jit(solution)/shard_map/all_gather | solution.py:67
  368.0 80.7 %all-gather.14.cloned.1.call-done = bf16[1024,2048]{1,0:T(8,128)(2,1)} async-done(((bf16[1024,512]{1,0:T(8,128)(2,1)}), bf16[1024,2048]{1,0:T(8,128)(2,1)}) %all-gather.14.cloned.1.call-update) | async-done | bytes 4194320 | tf_op jit(solution)/shard_map/all_gather | solution.py:71
  448.6 15.2 %convert_bitcast_fusion = bf16[2048,8,128]{0,2,1:T(8,128)(2,1)} fusion(bf16[1024,2048]{1,0:T(8,128)(2,1)} %all-gather.14.cloned.1.call-done, f32[8,128,1024]{2,1,0:T(8,128)} %fusion.8, bf16[2048,1024]{1,0:T(8,128)(2,1)} %all-gather.12.cloned.1.call-done, bf16[8,2048,128]{1,2,0:T(8,128)(2,1)} %all-gather.8.cloned.1.call-done, f32[2048]{0:T(1024)S(1)} %copy-done.2, ...), kind=kOutput, calls=%fused_computation.12 | convolution fusion | flops 8606711808 | bytes 20983808 | tf_op jit(solution)/shard_map/ucf,fk->kuc/dot_general | solution.py:73
  463.9 49.7 %reduce-scatter.5.cloned.1.call-done = bf16[256,8,128]{0,2,1:T(8,128)(2,1)} async-done(((bf16[2048,8,128]{0,2,1:T(8,128)(2,1)}), bf16[256,8,128]{0,2,1:T(8,128)(2,1)}) %reduce-scatter.5.cloned.1.call-update) | async-done | bytes 524304 | tf_op jit(solution)/shard_map/reduce_scatter | solution.py:72
  (34 shorter events, 16.3 us)
Async XLA Ops:
  6.5 32.1 %copy-start = (bf16[256,2048]{1,0:T(8,128)(2,1)S(1)}, bf16[256,2048]{1,0:T(8,128)(2,1)}, u32[]{:S(2)}) copy-start(bf16[256,2048]{1,0:T(8,128)(2,1)} %param.11) | copy-start | bytes 3145732
  6.5 125.4 %reduce-scatter.3.cloned.1.call-start = ((), (), s32[]{:S(2)}) async-start(), calls=%async_computation.2 | async-start | bytes 4718592 | tf_op jit(solution)/shard_map/reduce_scatter | solution.py:46
  6.5 10.4 %collective-permute-start = (bf16[8,256,128]{2,1,0:T(8,128)(2,1)}, bf16[8,256,128]{2,1,0:T(8,128)(2,1)S(1)}, u32[]{:S(2)}, u32[]{:S(2)}) collective-permute-start(bf16[8,256,128]{2,1,0:T(8,128)(2,1)} %param.9), channel_id=1, source_target_pairs={{0,7},{1,0},{2,1},{3,2},{4,3},{5,4},{6,5},{7,6},{8,15},{9,8},{10,9... | collective-permute-start | bytes 1572872 | tf_op jit(solution)/shard_map/ppermute | solution.py:30
  16.9 9.4 %collective-permute-start.1 = (bf16[8,256,128]{2,1,0:T(8,128)(2,1)S(1)}, bf16[8,256,128]{2,1,0:T(8,128)(2,1)S(1)}, u32[]{:S(2)}, u32[]{:S(2)}) collective-permute-start(bf16[8,256,128]{2,1,0:T(8,128)(2,1)S(1)} %collective-permute-done), channel_id=1, source_target_pairs={{0,7},{1,0},{2,1},{3,2},{4,3},{5,4},{6,5},{7,6},{8,15},{9,8},{10,9... | collective-permute-start | bytes 1572872 | tf_op jit(solution)/shard_map/ppermute | solution.py:30
  26.3 9.5 %collective-permute-start.2 = (bf16[8,256,128]{2,1,0:T(8,128)(2,1)S(1)}, bf16[8,256,128]{2,1,0:T(8,128)(2,1)S(1)}, u32[]{:S(2)}, u32[]{:S(2)}) collective-permute-start(bf16[8,256,128]{2,1,0:T(8,128)(2,1)S(1)} %collective-permute-done.1), channel_id=1, source_target_pairs={{0,7},{1,0},{2,1},{3,2},{4,3},{5,4},{6,5},{7,6},{8,15},{9,8},{10,9... | collective-permute-start | bytes 1572872 | tf_op jit(solution)/shard_map/ppermute | solution.py:30
  35.8 9.5 %collective-permute-start.3 = (bf16[8,256,128]{2,1,0:T(8,128)(2,1)S(1)}, bf16[8,256,128]{2,1,0:T(8,128)(2,1)S(1)}, u32[]{:S(2)}, u32[]{:S(2)}) collective-permute-start(bf16[8,256,128]{2,1,0:T(8,128)(2,1)S(1)} %collective-permute-done.2), channel_id=1, source_target_pairs={{0,7},{1,0},{2,1},{3,2},{4,3},{5,4},{6,5},{7,6},{8,15},{9,8},{10,9... | collective-permute-start | bytes 1572872 | tf_op jit(solution)/shard_map/ppermute | solution.py:30
  45.3 9.5 %collective-permute-start.4 = (bf16[8,256,128]{2,1,0:T(8,128)(2,1)S(1)}, bf16[8,256,128]{2,1,0:T(8,128)(2,1)S(1)}, u32[]{:S(2)}, u32[]{:S(2)}) collective-permute-start(bf16[8,256,128]{2,1,0:T(8,128)(2,1)S(1)} %collective-permute-done.3), channel_id=1, source_target_pairs={{0,7},{1,0},{2,1},{3,2},{4,3},{5,4},{6,5},{7,6},{8,15},{9,8},{10,9... | collective-permute-start | bytes 1572872 | tf_op jit(solution)/shard_map/ppermute | solution.py:30
  54.8 9.5 %collective-permute-start.5 = (bf16[8,256,128]{2,1,0:T(8,128)(2,1)S(1)}, bf16[8,256,128]{2,1,0:T(8,128)(2,1)S(1)}, u32[]{:S(2)}, u32[]{:S(2)}) collective-permute-start(bf16[8,256,128]{2,1,0:T(8,128)(2,1)S(1)} %collective-permute-done.4), channel_id=1, source_target_pairs={{0,7},{1,0},{2,1},{3,2},{4,3},{5,4},{6,5},{7,6},{8,15},{9,8},{10,9... | collective-permute-start | bytes 1572872 | tf_op jit(solution)/shard_map/ppermute | solution.py:30
  64.3 9.5 %collective-permute-start.6 = (bf16[8,256,128]{2,1,0:T(8,128)(2,1)S(1)}, bf16[8,256,128]{2,1,0:T(8,128)(2,1)S(1)}, u32[]{:S(2)}, u32[]{:S(2)}) collective-permute-start(bf16[8,256,128]{2,1,0:T(8,128)(2,1)S(1)} %collective-permute-done.5), channel_id=1, source_target_pairs={{0,7},{1,0},{2,1},{3,2},{4,3},{5,4},{6,5},{7,6},{8,15},{9,8},{10,9... | collective-permute-start | bytes 1572872 | tf_op jit(solution)/shard_map/ppermute | solution.py:30
  79.0 0.7 copy-start.1
  79.0 83.4 %all-gather.6.cloned.1.call-start = ((), (), s32[]{:S(2)}) async-start(), calls=%async_computation.3 | async-start | bytes 2359296 | tf_op jit(solution)/shard_map/all_gather | solution.py:48
  134.5 70.6 %all-gather.8.cloned.1.call-start = ((), (), s32[]{:S(2)}) async-start(), calls=%async_computation.4 | async-start | bytes 4718592 | tf_op jit(solution)/shard_map/all_gather | solution.py:52
  167.6 119.7 %copy-start.2 = (f32[2048]{0:T(1024)S(1)}, f32[2048]{0:T(1024)}, u32[]{:S(2)}) copy-start(f32[2048]{0:T(1024)} %param.12) | copy-start | bytes 24580
  167.6 119.7 %all-gather.10.cloned.1.call-start = ((), (), s32[]{:S(2)}) async-start(), calls=%async_computation.5 | async-start | bytes 5242880 | tf_op jit(solution)/shard_map/all_gather | solution.py:61
  168.2 199.8 %all-gather.12.cloned.1.call-start = ((), (), s32[]{:S(2)}) async-start(), calls=%async_computation.6 | async-start | bytes 5242880 | tf_op jit(solution)/shard_map/all_gather | solution.py:67
  168.8 279.9 %all-gather.14.cloned.1.call-start = ((), (), s32[]{:S(2)}) async-start(), calls=%async_computation.7 | async-start | bytes 5242880 | tf_op jit(solution)/shard_map/all_gather | solution.py:71
  169.3 344.2 %reduce-scatter.5.cloned.1.call-start = ((), (), s32[]{:S(2)}) async-start(), calls=%async_computation.8 | async-start | bytes 4718592 | tf_op jit(solution)/shard_map/reduce_scatter | solution.py:72
Sparse Core Ops, SparseCore 0:
  79.2 52.7 reduce-scatter.2
  134.6 27.7 all-gather.5
  167.7 37.3 all-gather.7
  206.5 80.7 all-gather.9
  288.7 79.2 all-gather.11
  369.4 79.2 all-gather.13
  464.0 49.5 reduce-scatter.4
